TPU v7x, 32 devices: a whole 2x2x4 slice. The times are simulated.
32 devices in a mesh: tm: 8 (over z, x), chan: 4 (over y, core).
Axes of the slice: x: 2, y: 2, z: 4, core: 2. Of those that a mesh axis runs over, the one named last changes fastest.
Arguments:
- record: float32 [8192, 1024], P('tm', 'chan'), may hold values from -120 to 120
- test_matrix: float32 [64, 1024, 128], P(None, 'chan'), may hold values from -0.0234375 to 0.0234375
Outputs:
- basis: float32 [8192, 128], P('tm')
- coeffs: float32 [64, 1024, 128], P('tm', 'chan')
All inputs are finite; a program needn't handle non-finite values.
Results may differ from a plain program's by a relative error of at most 0.00024.
Values sent between devices are 32-bit elements; how exact they have to be, the bound alone decides.
No kernel may reach another device: no remote copies, remote signals or barrier semaphores. Data moves between devices by JAX's collectives and lax.ppermute only.
A program may use at most 256 MiB of HBM per device.

v0:
```python
import math
import jax
import jax.numpy as jnp
from jax import lax
from jax.sharding import PartitionSpec as P

L = 64


def passed_along(block, axis, distance):
    devices = range(lax.axis_size(axis))
    route = [(i - distance, i) for i in devices if i - distance in devices]
    return lax.ppermute(block, axis, route)


def sketch_part(extended, test_local, rows):
    hi = lax.Precision.HIGHEST
    chans = test_local.shape[1]
    width = test_local.shape[2]
    total = jnp.zeros((rows, width), jnp.float32)
    for group in range(L // 8):
        block = jnp.concatenate(
            [extended[group * 8 + j : group * 8 + j + rows] for j in range(8)], axis=1
        )
        weights = test_local[group * 8 : (group + 1) * 8].reshape(8 * chans, width)
        total = total + jnp.dot(block, weights, precision=hi, preferred_element_type=jnp.float32)
    return total


def on_device(record, test_matrix):
    hi = lax.Precision.HIGHEST
    rows = record.shape[0]
    chans = record.shape[1]
    width = test_matrix.shape[2]
    n_time = lax.axis_size("tm")
    total_rows = rows * n_time
    rim = passed_along(record[: L - 1], "tm", -1)
    extended = jnp.concatenate([record, rim], axis=0)
    partial_value = sketch_part(extended, test_matrix, rows)
    own = lax.psum_scatter(partial_value, "chan", scatter_dimension=0, tiled=True)
    gram = jnp.dot(own.T, own, precision=hi, preferred_element_type=jnp.float32)
    lower = jnp.linalg.cholesky(lax.psum(gram, ("tm", "chan")))
    root = jnp.sqrt(jnp.float32(total_rows))
    share = (
        lax.linalg.triangular_solve(lower, own, left_side=False, lower=True, transpose_a=True)
        * root
    )
    basis = lax.all_gather(share, "chan", axis=0, tiled=True)
    scale = 1.0 / root
    start = jnp.int32(0)
    group = math.gcd(lax.axis_size("tm") * (L // n_time), 8)
    pieces = []
    for first in range(0, lax.axis_size("tm") * (L // n_time), group):
        block = jnp.concatenate(
            [lax.dynamic_slice_in_dim(extended, start + first + j, rows, 0) for j in range(group)],
            axis=1,
        )
        term = lax.dot_general(
            block, basis, (((0,), (0,)), ((), ())), precision=hi, preferred_element_type=jnp.float32
        )
        pieces.append(term.reshape(group, chans, width))
    coeffs = lax.psum_scatter(
        jnp.concatenate(pieces, axis=0) * scale, "tm", scatter_dimension=0, tiled=True
    )
    return (basis, coeffs)


def solution(mesh):
    placed = (P("tm", "chan"), P(None, "chan", None))
    return jax.shard_map(
        on_device,
        mesh=mesh,
        in_specs=placed,
        out_specs=(P("tm", None), P("tm", "chan", None)),
        check_vma=False,
    )
```

profile of v0, /device:TPU:0, one launch (start us, length us, event | category | flops | bytes accessed | tf_op | source)
XLA Modules:
  0.0 572.7 jit_solution(13978210390161302283)
XLA Ops:
  9.5 5.8 %fusion.9 = (f32[8,256,128]{2,1,0:T(8,128)}, f32[8,256,128]{2,1,0:T(8,128)S(1)}, f32[8,256,128]{2,1,0:T(8,128)S(1)}, f32[8,256,128]{2,1,0:T(8,128)}, f32[8,256,1...) fusion(f32[64,256,128]{2,1,0:T(8,128)} %param.3), kind=kLoop, calls=%fused_computation.92 | loop fusion | bytes 16777216 | tf_op jit(solution)/shard_map/slice | solution.py:25
  16.5 2.5 slice_dynamic-update-slice_fusion.55
  19.0 2.8 slice_dynamic-update-slice_fusion.62
  21.8 2.7 slice_dynamic-update-slice_fusion.61
  24.5 2.7 slice_dynamic-update-slice_fusion.60
  27.2 2.8 slice_dynamic-update-slice_fusion.59
  30.0 2.8 slice_dynamic-update-slice_fusion.58
  32.8 2.9 slice_dynamic-update-slice_fusion.57
  35.7 2.9 slice_dynamic-update-slice_fusion.56
  38.6 19.3 %fusion.10 = f32[1024,128]{1,0:T(8,128)S(1)} fusion(f32[1024,2048]{1,0:T(8,128)S(1)} %get-tuple-element.17, f32[2048,128]{1,0:T(8,128)} %bitcast.94), kind=kOutput, calls=%fused_computation.93 | convolution fusion | flops 3221225472 | bytes 9961472 | tf_op jit(solution)/shard_map/dot_general | solution.py:26
  58.0 9.2 %fusion.11 = f32[1024,128]{1,0:T(8,128)S(1)} fusion(f32[1024,2048]{1,0:T(8,128)} %get-tuple-element.16, f32[2048,128]{1,0:T(8,128)S(1)} %bitcast.93), kind=kOutput, calls=%fused_computation.94 | convolution fusion | flops 3221225472 | bytes 9961472 | tf_op jit(solution)/shard_map/dot_general | solution.py:26
  67.2 6.7 %fusion.12 = f32[1024,128]{1,0:T(8,128)S(1)} fusion(f32[1024,2048]{1,0:T(8,128)S(1)} %copy-done.2, f32[2048,128]{1,0:T(8,128)S(1)} %bitcast.92), kind=kOutput, calls=%fused_computation.95 | convolution fusion | flops 3221225472 | bytes 9961472 | tf_op jit(solution)/shard_map/dot_general | solution.py:26
  73.9 9.6 %fusion.13 = f32[1024,128]{1,0:T(8,128)S(1)} fusion(f32[1024,2048]{1,0:T(8,128)} %get-tuple-element.14, f32[2048,128]{1,0:T(8,128)S(1)} %bitcast.91), kind=kOutput, calls=%fused_computation.96 | convolution fusion | flops 3221225472 | bytes 9961472 | tf_op jit(solution)/shard_map/dot_general | solution.py:26
  83.6 6.7 %fusion.14 = f32[1024,128]{1,0:T(8,128)S(1)} fusion(f32[1024,2048]{1,0:T(8,128)S(1)} %bitcast.67, f32[2048,128]{1,0:T(8,128)S(1)} %bitcast.90), kind=kOutput, calls=%fused_computation.97 | convolution fusion | flops 3221225472 | bytes 9961472 | tf_op jit(solution)/shard_map/dot_general | solution.py:26
  90.3 6.9 %fusion.15 = f32[1024,128]{1,0:T(8,128)S(1)} fusion(f32[1024,2048]{1,0:T(8,128)S(1)} %bitcast.63, f32[2048,128]{1,0:T(8,128)S(1)} %bitcast.89), kind=kOutput, calls=%fused_computation.98 | convolution fusion | flops 3221225472 | bytes 9961472 | tf_op jit(solution)/shard_map/dot_general | solution.py:26
  97.2 6.7 %fusion.16 = f32[1024,128]{1,0:T(8,128)S(1)} fusion(f32[1024,2048]{1,0:T(8,128)S(1)} %get-tuple-element.11, f32[2048,128]{1,0:T(8,128)S(1)} %bitcast.88), kind=kOutput, calls=%fused_computation.99 | convolution fusion | flops 3221225472 | bytes 9961472 | tf_op jit(solution)/shard_map/dot_general | solution.py:26
  104.0 8.5 %fusion.5 = f32[1024,128]{1,0:T(8,128)} fusion(f32[1024,128]{1,0:T(8,128)S(1)} %fusion.16, f32[1024,128]{1,0:T(8,128)S(1)} %fusion.15, f32[1024,128]{1,0:T(8,128)S(1)} %fusion.14, f32[1024,128]{1,0:T(8,128)S(1)} %fusion.13, f32[1024,128]{1,0:T(8,128)S(1)} %fusion.12, f32[1024,128]{1,0:T(8,128)S(1)} %fusion.11, f32[1024,128]{1,0:T(8,128)S(1)} %fusion.10, ...), kind=kOutput, calls=%fused_computation.7 | convolution fusion | flops 3222142976 | bytes 13631488 | tf_op jit(solution)/shard_map/dot_general | solution.py:26
  112.5 25.6 %reduce-scatter.3.cloned.1.call-done = f32[256,128]{1,0:T(8,128)} async-done(((f32[1024,128]{1,0:T(8,128)}), f32[256,128]{1,0:T(8,128)}) %reduce-scatter.3.cloned.1.call-update) | async-done | bytes 131088 | tf_op jit(solution)/shard_map/reduce_scatter | solution.py:40
  140.2 123.5 %all-reduce.2.cloned.1.call-done = f32[128,128]{0,1:T(8,128)} async-done(((f32[128,128]{0,1:T(8,128)}), f32[128,128]{0,1:T(8,128)}) %all-reduce.2.cloned.1.call-update) | async-done | bytes 65552 | tf_op jit(solution)/shard_map/psum | solution.py:42
  265.5 11.7 %cholesky.16 = f32[128,128]{1,0:T(8,128)S(1)} custom-call(f32[128,128]{1,0:T(8,128)S(1)} %fusion.8), custom_call_target="Cholesky" | custom-call | tf_op jit(solution)/shard_map/jit(cholesky)/cholesky | solution.py:42
  278.5 9.8 %custom-call.6 = f32[1,128,128]{1,2,0:T(8,128)S(1)} custom-call(f32[1,128,128]{2,1,0:T(8,128)S(1)} %fusion.6), custom_call_target="InvertDiagBlocksLowerTriangular" | custom-call | tf_op jit(solution)/shard_map/triangular_solve | solution.py:45
  289.5 8.8 %all_gather.3 = f32[1024,128]{1,0:T(8,128)S(1)} all-gather(f32[256,128]{1,0:T(8,128)S(1)} %convolution_multiply_fusion), channel_id=1, replica_groups=mesh['tm'=8,'chan'=4] {'chan'}, dimensions={0}, use_global_device_ids=true | all-gather | bytes 655360 | tf_op jit(solution)/shard_map/all_gather | solution.py:48
  298.3 15.9 %fusion.25 = f32[2048,128]{1,0:T(8,128)S(1)} fusion(f32[1024,2048]{1,0:T(8,128)} %copy-done.1, f32[1024,128]{1,0:T(8,128)S(1)} %all_gather.3), kind=kOutput, calls=%fused_computation.108 | convolution fusion | flops 3221225472 | bytes 9961472 | tf_op jit(solution)/shard_map/dot_general | solution.py:58
  314.2 14.2 %fusion.24 = f32[2048,128]{1,0:T(8,128)S(1)} fusion(f32[1024,2048]{1,0:T(8,128)S(1)} %bitcast.65, f32[1024,128]{1,0:T(8,128)S(1)} %all_gather.3), kind=kOutput, calls=%fused_computation.107 | convolution fusion | flops 3221225472 | bytes 9961472 | tf_op jit(solution)/shard_map/dot_general | solution.py:58
  328.5 14.4 %fusion.23 = f32[2048,128]{1,0:T(8,128)S(1)} fusion(f32[1024,2048]{1,0:T(8,128)S(1)} %bitcast.69, f32[1024,128]{1,0:T(8,128)S(1)} %all_gather.3), kind=kOutput, calls=%fused_computation.106 | convolution fusion | flops 3221225472 | bytes 9961472 | tf_op jit(solution)/shard_map/dot_general | solution.py:58
  343.0 14.2 %fusion.22 = f32[2048,128]{1,0:T(8,128)S(1)} fusion(f32[1024,2048]{1,0:T(8,128)S(1)} %bitcast.71, f32[1024,128]{1,0:T(8,128)S(1)} %all_gather.3), kind=kOutput, calls=%fused_computation.105 | convolution fusion | flops 3221225472 | bytes 9961472 | tf_op jit(solution)/shard_map/dot_general | solution.py:58
  357.2 14.2 %fusion.21 = f32[2048,128]{1,0:T(8,128)S(1)} fusion(f32[1024,2048]{1,0:T(8,128)S(1)} %bitcast.73, f32[1024,128]{1,0:T(8,128)S(1)} %all_gather.3), kind=kOutput, calls=%fused_computation.104 | convolution fusion | flops 3221225472 | bytes 9961472 | tf_op jit(solution)/shard_map/dot_general | solution.py:58
  371.5 14.4 %fusion.20 = f32[2048,128]{1,0:T(8,128)S(1)} fusion(f32[1024,2048]{1,0:T(8,128)S(1)} %bitcast.75, f32[1024,128]{1,0:T(8,128)S(1)} %all_gather.3), kind=kOutput, calls=%fused_computation.103 | convolution fusion | flops 3221225472 | bytes 9961472 | tf_op jit(solution)/shard_map/dot_general | solution.py:58
  386.0 13.9 %fusion.19 = f32[2048,128]{1,0:T(8,128)S(1)} fusion(f32[1024,2048]{1,0:T(8,128)S(1)} %bitcast.61, f32[1024,128]{1,0:T(8,128)S(1)} %all_gather.3), kind=kOutput, calls=%fused_computation.102 | convolution fusion | flops 3221225472 | bytes 9961472 | tf_op jit(solution)/shard_map/dot_general | solution.py:58
  399.9 14.0 %fusion.18 = f32[2048,128]{1,0:T(8,128)S(1)} fusion(f32[1024,2048]{1,0:T(8,128)S(1)} %bitcast.79, f32[1024,128]{1,0:T(8,128)S(1)} %all_gather.3), kind=kOutput, calls=%fused_computation.101 | convolution fusion | flops 3221225472 | bytes 9961472 | tf_op jit(solution)/shard_map/dot_general | solution.py:58
  414.5 4.1 broadcast_multiply_fusion
  418.6 146.5 %reduce-scatter.5.cloned.1.call-done = f32[8,256,128]{2,1,0:T(8,128)} async-done(((f32[64,256,128]{2,1,0:T(8,128)}), f32[8,256,128]{2,1,0:T(8,128)}) %reduce-scatter.5.cloned.1.call-update) | async-done | bytes 1048592 | tf_op jit(solution)/shard_map/reduce_scatter | solution.py:62
  (91 shorter events, 11.4 us)
Async XLA Ops:
  7.2 131.0 %reduce-scatter.3.cloned.1.call-start = ((), (), s32[]{:S(2)}) async-start(), calls=%async_computation.2 | async-start | bytes 655360 | tf_op jit(solution)/shard_map/reduce_scatter | solution.py:40
  8.1 7.3 %copy-start.6 = (f32[1024,256]{1,0:T(8,128)S(1)}, f32[1024,256]{1,0:T(8,128)}, u32[]{:S(2)}) copy-start(f32[1024,256]{1,0:T(8,128)} %param.2) | copy-start | bytes 3145732
  8.1 8.4 %collective-permute-start = (f32[63,256]{1,0:T(8,128)S(1)}, f32[63,256]{1,0:T(8,128)S(1)}, u32[]{:S(2)}, u32[]{:S(2)}) collective-permute-start(f32[63,256]{1,0:T(8,128)S(1)} %slice.226), channel_id=1, source_target_pairs={{4,0},{8,4},{12,8},{16,12},{20,16},{24,20},{28,24},{5,1},{9,5},{13... | collective-permute-start | bytes 193544 | tf_op jit(solution)/shard_map/ppermute | solution.py:13
  38.6 28.6 %copy-start = (f32[1024,2048]{1,0:T(8,128)}, f32[1024,2048]{1,0:T(8,128)S(1)}, u32[]{:S(2)}) copy-start(f32[1024,2048]{1,0:T(8,128)S(1)} %get-tuple-element.17) | copy-start | bytes 25165828
  38.6 58.6 %copy-start.1 = (f32[1024,2048]{1,0:T(8,128)}, f32[1024,2048]{1,0:T(8,128)S(1)}, u32[]{:S(2)}) copy-start(f32[1024,2048]{1,0:T(8,128)S(1)} %get-tuple-element.11) | copy-start | bytes 25165828
  38.6 19.3 %copy-start.4 = (f32[8,256,128]{2,1,0:T(8,128)S(1)}, f32[8,256,128]{2,1,0:T(8,128)}, u32[]{:S(2)}) copy-start(f32[8,256,128]{2,1,0:T(8,128)} %get-tuple-element.6) | copy-start | bytes 3145732
  38.6 28.6 %copy-start.3 = (f32[8,256,128]{2,1,0:T(8,128)S(1)}, f32[8,256,128]{2,1,0:T(8,128)}, u32[]{:S(2)}) copy-start(f32[8,256,128]{2,1,0:T(8,128)} %get-tuple-element.5) | copy-start | bytes 3145732
  57.9 9.3 %copy-start.2 = (f32[1024,2048]{1,0:T(8,128)S(1)}, f32[1024,2048]{1,0:T(8,128)}, u32[]{:S(2)}) copy-start(f32[1024,2048]{1,0:T(8,128)} %get-tuple-element.15) | copy-start | bytes 25165828
  58.0 25.6 %slice-start.6 = ((s8[8388608]{0:T(1024)(128)(4,1)}), s8[4194304]{0:T(1024)(128)(4,1)S(1)}, s32[]{:S(2)}) async-start(s8[8388608]{0:T(1024)(128)(4,1)} %bitcast.66), calls=%async_computation.11 | async-start | bytes 8388608
  67.2 16.4 %slice-start.7 = ((s8[8388608]{0:T(1024)(128)(4,1)}), s8[4194304]{0:T(1024)(128)(4,1)S(1)}, s32[]{:S(2)}) async-start(s8[8388608]{0:T(1024)(128)(4,1)} %bitcast.66), calls=%async_computation.12 | async-start | bytes 8388608
  73.9 16.4 %slice-start.2 = ((s8[8388608]{0:T(1024)(128)(4,1)}), s8[4194304]{0:T(1024)(128)(4,1)S(1)}, s32[]{:S(2)}) async-start(s8[8388608]{0:T(1024)(128)(4,1)} %bitcast.62), calls=%async_computation.7 | async-start | bytes 8388608
  83.6 6.7 %slice-start.3 = ((s8[8388608]{0:T(1024)(128)(4,1)}), s8[4194304]{0:T(1024)(128)(4,1)S(1)}, s32[]{:S(2)}) async-start(s8[8388608]{0:T(1024)(128)(4,1)} %bitcast.62), calls=%async_computation.8 | async-start | bytes 8388608
  90.3 13.6 %slice-start.16 = ((s8[8388608]{0:T(1024)(128)(4,1)}), s8[4194304]{0:T(1024)(128)(4,1)S(1)}, s32[]{:S(2)}) async-start(s8[8388608]{0:T(1024)(128)(4,1)} %bitcast.76), calls=%async_computation.21 | async-start | bytes 8388608
  90.3 13.6 %copy-start.5 = (f32[8,256,128]{2,1,0:T(8,128)S(1)}, f32[8,256,128]{2,1,0:T(8,128)}, u32[]{:S(2)}) copy-start(f32[8,256,128]{2,1,0:T(8,128)} %get-tuple-element.2) | copy-start | bytes 3145732
  97.2 6.7 %slice-start.17 = ((s8[8388608]{0:T(1024)(128)(4,1)}), s8[4194304]{0:T(1024)(128)(4,1)S(1)}, s32[]{:S(2)}) async-start(s8[8388608]{0:T(1024)(128)(4,1)} %bitcast.76), calls=%async_computation.22 | async-start | bytes 8388608
  112.5 151.2 %all-reduce.2.cloned.1.call-start = ((), (), s32[]{:S(2)}) async-start(), calls=%async_computation.3 | async-start | bytes 131072 | tf_op jit(solution)/shard_map/psum | solution.py:42
  140.2 425.0 %reduce-scatter.5.cloned.1.call-start = ((), (), s32[]{:S(2)}) async-start(), calls=%async_computation.4 | async-start | bytes 9437184 | tf_op jit(solution)/shard_map/reduce_scatter | solution.py:62
  289.5 24.7 %slice-start.4 = ((s8[8388608]{0:T(1024)(128)(4,1)}), s8[4194304]{0:T(1024)(128)(4,1)S(1)}, s32[]{:S(2)}) async-start(s8[8388608]{0:T(1024)(128)(4,1)} %bitcast.64), calls=%async_computation.9 | async-start | bytes 8388608
  298.3 15.9 %slice-start.5 = ((s8[8388608]{0:T(1024)(128)(4,1)}), s8[4194304]{0:T(1024)(128)(4,1)S(1)}, s32[]{:S(2)}) async-start(s8[8388608]{0:T(1024)(128)(4,1)} %bitcast.64), calls=%async_computation.10 | async-start | bytes 8388608
  298.3 30.2 %slice-start.8 = ((s8[8388608]{0:T(1024)(128)(4,1)}), s8[4194304]{0:T(1024)(128)(4,1)S(1)}, s32[]{:S(2)}) async-start(s8[8388608]{0:T(1024)(128)(4,1)} %bitcast.68), calls=%async_computation.13 | async-start | bytes 8388608
  314.2 14.3 %slice-start.9 = ((s8[8388608]{0:T(1024)(128)(4,1)}), s8[4194304]{0:T(1024)(128)(4,1)S(1)}, s32[]{:S(2)}) async-start(s8[8388608]{0:T(1024)(128)(4,1)} %bitcast.68), calls=%async_computation.14 | async-start | bytes 8388608
  314.2 28.7 %slice-start.10 = ((s8[8388608]{0:T(1024)(128)(4,1)}), s8[4194304]{0:T(1024)(128)(4,1)S(1)}, s32[]{:S(2)}) async-start(s8[8388608]{0:T(1024)(128)(4,1)} %bitcast.70), calls=%async_computation.15 | async-start | bytes 8388608
  328.5 14.5 %slice-start.11 = ((s8[8388608]{0:T(1024)(128)(4,1)}), s8[4194304]{0:T(1024)(128)(4,1)S(1)}, s32[]{:S(2)}) async-start(s8[8388608]{0:T(1024)(128)(4,1)} %bitcast.70), calls=%async_computation.16 | async-start | bytes 8388608
  328.5 28.7 %slice-start.12 = ((s8[8388608]{0:T(1024)(128)(4,1)}), s8[4194304]{0:T(1024)(128)(4,1)S(1)}, s32[]{:S(2)}) async-start(s8[8388608]{0:T(1024)(128)(4,1)} %bitcast.72), calls=%async_computation.17 | async-start | bytes 8388608
  343.0 14.2 %slice-start.13 = ((s8[8388608]{0:T(1024)(128)(4,1)}), s8[4194304]{0:T(1024)(128)(4,1)S(1)}, s32[]{:S(2)}) async-start(s8[8388608]{0:T(1024)(128)(4,1)} %bitcast.72), calls=%async_computation.18 | async-start | bytes 8388608
  343.0 28.5 %slice-start.14 = ((s8[8388608]{0:T(1024)(128)(4,1)}), s8[4194304]{0:T(1024)(128)(4,1)S(1)}, s32[]{:S(2)}) async-start(s8[8388608]{0:T(1024)(128)(4,1)} %bitcast.74), calls=%async_computation.19 | async-start | bytes 8388608
  357.2 14.3 %slice-start.15 = ((s8[8388608]{0:T(1024)(128)(4,1)}), s8[4194304]{0:T(1024)(128)(4,1)S(1)}, s32[]{:S(2)}) async-start(s8[8388608]{0:T(1024)(128)(4,1)} %bitcast.74), calls=%async_computation.20 | async-start | bytes 8388608
  357.2 28.7 %slice-start = ((s8[8388608]{0:T(1024)(128)(4,1)}), s8[4194304]{0:T(1024)(128)(4,1)S(1)}, s32[]{:S(2)}) async-start(s8[8388608]{0:T(1024)(128)(4,1)} %bitcast.60), calls=%async_computation.5 | async-start | bytes 8388608
  371.5 14.5 %slice-start.1 = ((s8[8388608]{0:T(1024)(128)(4,1)}), s8[4194304]{0:T(1024)(128)(4,1)S(1)}, s32[]{:S(2)}) async-start(s8[8388608]{0:T(1024)(128)(4,1)} %bitcast.60), calls=%async_computation.6 | async-start | bytes 8388608
  371.5 28.4 %slice-start.18 = ((s8[8388608]{0:T(1024)(128)(4,1)}), s8[4194304]{0:T(1024)(128)(4,1)S(1)}, s32[]{:S(2)}) async-start(s8[8388608]{0:T(1024)(128)(4,1)} %bitcast.78), calls=%async_computation.23 | async-start | bytes 8388608
  385.9 13.9 %slice-start.19 = ((s8[8388608]{0:T(1024)(128)(4,1)}), s8[4194304]{0:T(1024)(128)(4,1)S(1)}, s32[]{:S(2)}) async-start(s8[8388608]{0:T(1024)(128)(4,1)} %bitcast.78), calls=%async_computation.24 | async-start | bytes 8388608
Sparse Core Ops, SparseCore 0:
  112.6 25.5 reduce-scatter.2
  144.3 119.3 all-reduce.1
  418.8 146.3 reduce-scatter.4
where the time goes:
time: 582 us; the launch traced here: 573 us
  waiting for transfers between devices  296 us (51%)
  matrix products  192 us (33%)
  local copies, waits for them, and re-layouts  32.4 us (6%)
  other arithmetic  27.8 us (5%)
  between operations  14.6 us (3%)
  blocking collectives  8.78 us (2%)
    reduce_scatter x1, waiting for transfers between devices, on_device(): lax.psum_scatter(jnp.concatenate(pieces, axis=0) * scale, 'tm', scatter_d...  147 us
    psum x1, waiting for transfers between devices, on_device(): lower = jnp.linalg.cholesky(lax.psum(gram, ('tm', 'chan')))  123 us
    dot_general x8, matrix products, on_device(): lax.dot_general(block, basis, (((0,), (0,)), ((), ())), precision=hi, pre...  115 us
    dot_general x8, matrix products, sketch_part(): jnp.dot(block, weights, precision=hi, preferred_element_type=jnp.float32)  73.6 us
    reduce_scatter x1, waiting for transfers between devices, on_device(): lax.psum_scatter(partial_value, 'chan', scatter_dimension=0, tiled=True)  25.6 us
    unnamed x70, local copies, waits for them, and re-layouts  21.8 us
    another operation x3, other arithmetic, on_device(): lower = jnp.linalg.cholesky(lax.psum(gram, ('tm', 'chan')))  12.4 us
  transfers between devices with their start and end apart: 4, of which 3 were waited for; matrix products, arithmetic and copies ran while one was open for 1% of the time, Pallas kernels for 0%

commit v1 on v0

--- a/solution.py
+++ b/solution.py
@@ -5,6 +5,12 @@
 from jax.sharding import PartitionSpec as P
 
 L = 64
+
+
+def side_note(mine_x):
+    for j0 in ("tm", "chan"):
+        mine_x = jax.lax.psum(mine_x, j0)
+    return mine_x
 
 
 def passed_along(block, axis, distance):
@@ -39,7 +45,7 @@
     partial_value = sketch_part(extended, test_matrix, rows)
     own = lax.psum_scatter(partial_value, "chan", scatter_dimension=0, tiled=True)
     gram = jnp.dot(own.T, own, precision=hi, preferred_element_type=jnp.float32)
-    lower = jnp.linalg.cholesky(lax.psum(gram, ("tm", "chan")))
+    lower = jnp.linalg.cholesky(side_note(gram))
     root = jnp.sqrt(jnp.float32(total_rows))
     share = (
         lax.linalg.triangular_solve(lower, own, left_side=False, lower=True, transpose_a=True)

time: 582 us -> 562 us (0.966)
  waiting for transfers between devices: 296 us -> 279 us
    psum x1 -> x2, waiting for transfers between devices: 123 us -> 105 us  [side_note(): mine_x = jax.lax.psum(mine_x, j0)]
    unnamed x70 -> x74, local copies, waits for them, and re-layouts: 21.8 us -> 21.9 us
  transfers between devices with their start and end apart: 4 -> 5, of which waited for: 3 -> 4; matrix products, arithmetic and copies ran while one was open for 1% -> 1% of each run, Pallas kernels for 0% -> 0%
where the time goes in v1:
time: 562 us; the launch traced here: 553 us
  waiting for transfers between devices  279 us (50%)
  matrix products  191 us (34%)
  local copies, waits for them, and re-layouts  32.3 us (6%)
  other arithmetic  27.8 us (5%)
  between operations  14.7 us (3%)
  blocking collectives  7.1 us (1%)
    reduce_scatter x1, waiting for transfers between devices, on_device(): lax.psum_scatter(jnp.concatenate(pieces, axis=0) * scale, 'tm', scatter_d...  148 us
    dot_general x8, matrix products, on_device(): lax.dot_general(block, basis, (((0,), (0,)), ((), ())), precision=hi, pre...  115 us
    psum x2, waiting for transfers between devices, side_note(): mine_x = jax.lax.psum(mine_x, j0)  105 us
    dot_general x8, matrix products, sketch_part(): jnp.dot(block, weights, precision=hi, preferred_element_type=jnp.float32)  72.2 us
    reduce_scatter x1, waiting for transfers between devices, on_device(): lax.psum_scatter(partial_value, 'chan', scatter_dimension=0, tiled=True)  25.6 us
    unnamed x74, local copies, waits for them, and re-layouts  21.9 us
    another operation x3, other arithmetic, on_device(): lower = jnp.linalg.cholesky(side_note(gram))  12.4 us
  transfers between devices with their start and end apart: 5, of which 4 were waited for; matrix products, arithmetic and copies ran while one was open for 1% of the time, Pallas kernels for 0%

profile of v1, /device:TPU:0, one launch (start us, length us, event | category | flops | bytes accessed | tf_op | source)
XLA Modules:
  0.0 553.0 jit_solution(3461954694918278827)
XLA Ops:
  9.5 5.8 %fusion.9 = (f32[8,256,128]{2,1,0:T(8,128)}, f32[8,256,128]{2,1,0:T(8,128)S(1)}, f32[8,256,128]{2,1,0:T(8,128)S(1)}, f32[8,256,128]{2,1,0:T(8,128)}, f32[8,256,1...) fusion(f32[64,256,128]{2,1,0:T(8,128)} %param.3), kind=kLoop, calls=%fused_computation.92 | loop fusion | bytes 16777216 | tf_op jit(solution)/shard_map/slice | solution.py:31
  18.9 2.8 slice_dynamic-update-slice_fusion.62
  21.7 2.9 slice_dynamic-update-slice_fusion.61
  24.6 2.9 slice_dynamic-update-slice_fusion.60
  27.5 2.8 slice_dynamic-update-slice_fusion.59
  30.3 2.9 slice_dynamic-update-slice_fusion.58
  33.2 2.7 slice_dynamic-update-slice_fusion.57
  35.8 2.7 slice_dynamic-update-slice_fusion.56
  38.6 20.2 %fusion.10 = f32[1024,128]{1,0:T(8,128)S(1)} fusion(f32[1024,2048]{1,0:T(8,128)S(1)} %get-tuple-element.17, f32[2048,128]{1,0:T(8,128)} %bitcast.94), kind=kOutput, calls=%fused_computation.93 | convolution fusion | flops 3221225472 | bytes 9961472 | tf_op jit(solution)/shard_map/dot_general | solution.py:32
  58.8 9.2 %fusion.11 = f32[1024,128]{1,0:T(8,128)S(1)} fusion(f32[1024,2048]{1,0:T(8,128)} %get-tuple-element.16, f32[2048,128]{1,0:T(8,128)S(1)} %bitcast.93), kind=kOutput, calls=%fused_computation.94 | convolution fusion | flops 3221225472 | bytes 9961472 | tf_op jit(solution)/shard_map/dot_general | solution.py:32
  68.1 7.5 %fusion.12 = f32[1024,128]{1,0:T(8,128)} fusion(f32[1024,2048]{1,0:T(8,128)S(1)} %copy-done.3, f32[2048,128]{1,0:T(8,128)S(1)} %bitcast.92), kind=kOutput, calls=%fused_computation.95 | convolution fusion | flops 3221225472 | bytes 9961472 | tf_op jit(solution)/shard_map/dot_general | solution.py:32
  75.6 7.1 %fusion.13 = f32[1024,128]{1,0:T(8,128)S(1)} fusion(f32[1024,2048]{1,0:T(8,128)S(1)} %copy-done.2, f32[2048,128]{1,0:T(8,128)S(1)} %bitcast.91), kind=kOutput, calls=%fused_computation.96 | convolution fusion | flops 3221225472 | bytes 9961472 | tf_op jit(solution)/shard_map/dot_general | solution.py:32
  82.7 6.7 %fusion.14 = f32[1024,128]{1,0:T(8,128)S(1)} fusion(f32[1024,2048]{1,0:T(8,128)S(1)} %bitcast.67, f32[2048,128]{1,0:T(8,128)S(1)} %bitcast.90), kind=kOutput, calls=%fused_computation.97 | convolution fusion | flops 3221225472 | bytes 9961472 | tf_op jit(solution)/shard_map/dot_general | solution.py:32
  89.4 6.9 %fusion.15 = f32[1024,128]{1,0:T(8,128)S(1)} fusion(f32[1024,2048]{1,0:T(8,128)S(1)} %bitcast.63, f32[2048,128]{1,0:T(8,128)S(1)} %bitcast.89), kind=kOutput, calls=%fused_computation.98 | convolution fusion | flops 3221225472 | bytes 9961472 | tf_op jit(solution)/shard_map/dot_general | solution.py:32
  96.3 6.7 %fusion.16 = f32[1024,128]{1,0:T(8,128)S(1)} fusion(f32[1024,2048]{1,0:T(8,128)S(1)} %get-tuple-element.11, f32[2048,128]{1,0:T(8,128)S(1)} %bitcast.88), kind=kOutput, calls=%fused_computation.99 | convolution fusion | flops 3221225472 | bytes 9961472 | tf_op jit(solution)/shard_map/dot_general | solution.py:32
  103.1 8.0 %fusion.5 = f32[1024,128]{1,0:T(8,128)} fusion(f32[1024,128]{1,0:T(8,128)S(1)} %fusion.16, f32[1024,128]{1,0:T(8,128)S(1)} %fusion.15, f32[1024,128]{1,0:T(8,128)S(1)} %fusion.14, f32[1024,128]{1,0:T(8,128)S(1)} %fusion.13, f32[1024,128]{1,0:T(8,128)S(1)} %copy-done.7, f32[1024,128]{1,0:T(8,128)S(1)} %fusion.11, f32[1024,128]{1,0:T(8,128)S(1)} %fusion.10, ...), kind=kOutput, calls=%fused_computation.7 | convolution fusion | flops 3222142976 | bytes 13631488 | tf_op jit(solution)/shard_map/dot_general | solution.py:32
  111.2 25.6 %reduce-scatter.3.cloned.1.call-done = f32[256,128]{1,0:T(8,128)} async-done(((f32[1024,128]{1,0:T(8,128)}), f32[256,128]{1,0:T(8,128)}) %reduce-scatter.3.cloned.1.call-update) | async-done | bytes 131088 | tf_op jit(solution)/shard_map/reduce_scatter | solution.py:46
  138.9 71.2 %all-reduce.3.cloned.1.call-done = f32[128,128]{0,1:T(8,128)} async-done(((f32[128,128]{0,1:T(8,128)}), f32[128,128]{0,1:T(8,128)}) %all-reduce.3.cloned.1.call-update) | async-done | bytes 65552 | tf_op jit(solution)/shard_map/psum | solution.py:12
  210.4 33.5 %all-reduce.5.cloned.1.call-done = f32[128,128]{0,1:T(8,128)} async-done(((f32[128,128]{0,1:T(8,128)}), f32[128,128]{0,1:T(8,128)}) %all-reduce.5.cloned.1.call-update) | async-done | bytes 65552 | tf_op jit(solution)/shard_map/psum | solution.py:12
  245.7 11.7 %cholesky.16 = f32[128,128]{1,0:T(8,128)S(1)} custom-call(f32[128,128]{1,0:T(8,128)S(1)} %fusion.8), custom_call_target="Cholesky" | custom-call | tf_op jit(solution)/shard_map/jit(cholesky)/cholesky | solution.py:48
  258.7 9.8 %custom-call.6 = f32[1,128,128]{1,2,0:T(8,128)S(1)} custom-call(f32[1,128,128]{2,1,0:T(8,128)S(1)} %fusion.6), custom_call_target="InvertDiagBlocksLowerTriangular" | custom-call | tf_op jit(solution)/shard_map/triangular_solve | solution.py:51
  269.7 7.1 %all_gather.3 = f32[1024,128]{1,0:T(8,128)S(1)} all-gather(f32[256,128]{1,0:T(8,128)S(1)} %convolution_multiply_fusion), channel_id=1, replica_groups=mesh['tm'=8,'chan'=4] {'chan'}, dimensions={0}, use_global_device_ids=true | all-gather | bytes 655360 | tf_op jit(solution)/shard_map/all_gather | solution.py:54
  276.8 15.9 %fusion.25 = f32[2048,128]{1,0:T(8,128)S(1)} fusion(f32[1024,2048]{1,0:T(8,128)} %copy-done.1, f32[1024,128]{1,0:T(8,128)S(1)} %all_gather.3), kind=kOutput, calls=%fused_computation.108 | convolution fusion | flops 3221225472 | bytes 9961472 | tf_op jit(solution)/shard_map/dot_general | solution.py:64
  292.8 14.2 %fusion.24 = f32[2048,128]{1,0:T(8,128)S(1)} fusion(f32[1024,2048]{1,0:T(8,128)S(1)} %bitcast.65, f32[1024,128]{1,0:T(8,128)S(1)} %all_gather.3), kind=kOutput, calls=%fused_computation.107 | convolution fusion | flops 3221225472 | bytes 9961472 | tf_op jit(solution)/shard_map/dot_general | solution.py:64
  307.0 14.4 %fusion.23 = f32[2048,128]{1,0:T(8,128)S(1)} fusion(f32[1024,2048]{1,0:T(8,128)S(1)} %bitcast.69, f32[1024,128]{1,0:T(8,128)S(1)} %all_gather.3), kind=kOutput, calls=%fused_computation.106 | convolution fusion | flops 3221225472 | bytes 9961472 | tf_op jit(solution)/shard_map/dot_general | solution.py:64
  321.5 14.2 %fusion.22 = f32[2048,128]{1,0:T(8,128)S(1)} fusion(f32[1024,2048]{1,0:T(8,128)S(1)} %bitcast.71, f32[1024,128]{1,0:T(8,128)S(1)} %all_gather.3), kind=kOutput, calls=%fused_computation.105 | convolution fusion | flops 3221225472 | bytes 9961472 | tf_op jit(solution)/shard_map/dot_general | solution.py:64
  335.7 14.2 %fusion.21 = f32[2048,128]{1,0:T(8,128)S(1)} fusion(f32[1024,2048]{1,0:T(8,128)S(1)} %bitcast.73, f32[1024,128]{1,0:T(8,128)S(1)} %all_gather.3), kind=kOutput, calls=%fused_computation.104 | convolution fusion | flops 3221225472 | bytes 9961472 | tf_op jit(solution)/shard_map/dot_general | solution.py:64
  350.0 14.4 %fusion.20 = f32[2048,128]{1,0:T(8,128)S(1)} fusion(f32[1024,2048]{1,0:T(8,128)S(1)} %bitcast.75, f32[1024,128]{1,0:T(8,128)S(1)} %all_gather.3), kind=kOutput, calls=%fused_computation.103 | convolution fusion | flops 3221225472 | bytes 9961472 | tf_op jit(solution)/shard_map/dot_general | solution.py:64
  364.5 13.9 %fusion.19 = f32[2048,128]{1,0:T(8,128)S(1)} fusion(f32[1024,2048]{1,0:T(8,128)S(1)} %bitcast.61, f32[1024,128]{1,0:T(8,128)S(1)} %all_gather.3), kind=kOutput, calls=%fused_computation.102 | convolution fusion | flops 3221225472 | bytes 9961472 | tf_op jit(solution)/shard_map/dot_general | solution.py:64
  378.4 14.0 %fusion.18 = f32[2048,128]{1,0:T(8,128)S(1)} fusion(f32[1024,2048]{1,0:T(8,128)S(1)} %bitcast.79, f32[1024,128]{1,0:T(8,128)S(1)} %all_gather.3), kind=kOutput, calls=%fused_computation.101 | convolution fusion | flops 3221225472 | bytes 9961472 | tf_op jit(solution)/shard_map/dot_general | solution.py:64
  393.0 4.1 broadcast_multiply_fusion
  397.2 148.3 %reduce-scatter.5.cloned.1.call-done = f32[8,256,128]{2,1,0:T(8,128)} async-done(((f32[64,256,128]{2,1,0:T(8,128)}), f32[8,256,128]{2,1,0:T(8,128)}) %reduce-scatter.5.cloned.1.call-update) | async-done | bytes 1048592 | tf_op jit(solution)/shard_map/reduce_scatter | solution.py:68
  (98 shorter events, 14.1 us)
Async XLA Ops:
  7.2 129.6 %reduce-scatter.3.cloned.1.call-start = ((), (), s32[]{:S(2)}) async-start(), calls=%async_computation.2 | async-start | bytes 655360 | tf_op jit(solution)/shard_map/reduce_scatter | solution.py:46
  8.1 7.2 %copy-start.8 = (f32[1024,256]{1,0:T(8,128)S(1)}, f32[1024,256]{1,0:T(8,128)}, u32[]{:S(2)}) copy-start(f32[1024,256]{1,0:T(8,128)} %param.2) | copy-start | bytes 3145732
  8.1 8.4 %collective-permute-start = (f32[63,256]{1,0:T(8,128)S(1)}, f32[63,256]{1,0:T(8,128)S(1)}, u32[]{:S(2)}, u32[]{:S(2)}) collective-permute-start(f32[63,256]{1,0:T(8,128)S(1)} %slice.226), channel_id=1, source_target_pairs={{4,0},{8,4},{12,8},{16,12},{20,16},{24,20},{28,24},{5,1},{9,5},{13... | collective-permute-start | bytes 193544 | tf_op jit(solution)/shard_map/ppermute | solution.py:19
  38.6 29.5 %copy-start = (f32[1024,2048]{1,0:T(8,128)}, f32[1024,2048]{1,0:T(8,128)S(1)}, u32[]{:S(2)}) copy-start(f32[1024,2048]{1,0:T(8,128)S(1)} %get-tuple-element.17) | copy-start | bytes 25165828
  38.6 57.8 %copy-start.1 = (f32[1024,2048]{1,0:T(8,128)}, f32[1024,2048]{1,0:T(8,128)S(1)}, u32[]{:S(2)}) copy-start(f32[1024,2048]{1,0:T(8,128)S(1)} %get-tuple-element.11) | copy-start | bytes 25165828
  38.6 20.2 %copy-start.5 = (f32[8,256,128]{2,1,0:T(8,128)S(1)}, f32[8,256,128]{2,1,0:T(8,128)}, u32[]{:S(2)}) copy-start(f32[8,256,128]{2,1,0:T(8,128)} %get-tuple-element.6) | copy-start | bytes 3145732
  38.6 29.5 %copy-start.4 = (f32[8,256,128]{2,1,0:T(8,128)S(1)}, f32[8,256,128]{2,1,0:T(8,128)}, u32[]{:S(2)}) copy-start(f32[8,256,128]{2,1,0:T(8,128)} %get-tuple-element.5) | copy-start | bytes 3145732
  58.8 9.3 %copy-start.3 = (f32[1024,2048]{1,0:T(8,128)S(1)}, f32[1024,2048]{1,0:T(8,128)}, u32[]{:S(2)}) copy-start(f32[1024,2048]{1,0:T(8,128)} %get-tuple-element.15) | copy-start | bytes 25165828
  58.8 23.9 %slice-start.6 = ((s8[8388608]{0:T(1024)(128)(4,1)}), s8[4194304]{0:T(1024)(128)(4,1)S(1)}, s32[]{:S(2)}) async-start(s8[8388608]{0:T(1024)(128)(4,1)} %bitcast.66), calls=%async_computation.12 | async-start | bytes 8388608
  68.1 7.5 %copy-start.2 = (f32[1024,2048]{1,0:T(8,128)S(1)}, f32[1024,2048]{1,0:T(8,128)}, u32[]{:S(2)}) copy-start(f32[1024,2048]{1,0:T(8,128)} %get-tuple-element.14) | copy-start | bytes 25165828
  68.1 14.6 %slice-start.7 = ((s8[8388608]{0:T(1024)(128)(4,1)}), s8[4194304]{0:T(1024)(128)(4,1)S(1)}, s32[]{:S(2)}) async-start(s8[8388608]{0:T(1024)(128)(4,1)} %bitcast.66), calls=%async_computation.13 | async-start | bytes 8388608
  75.6 13.8 %slice-start.2 = ((s8[8388608]{0:T(1024)(128)(4,1)}), s8[4194304]{0:T(1024)(128)(4,1)S(1)}, s32[]{:S(2)}) async-start(s8[8388608]{0:T(1024)(128)(4,1)} %bitcast.62), calls=%async_computation.8 | async-start | bytes 8388608
  89.4 13.6 %slice-start.16 = ((s8[8388608]{0:T(1024)(128)(4,1)}), s8[4194304]{0:T(1024)(128)(4,1)S(1)}, s32[]{:S(2)}) async-start(s8[8388608]{0:T(1024)(128)(4,1)} %bitcast.76), calls=%async_computation.22 | async-start | bytes 8388608
  89.4 13.6 %copy-start.6 = (f32[8,256,128]{2,1,0:T(8,128)S(1)}, f32[8,256,128]{2,1,0:T(8,128)}, u32[]{:S(2)}) copy-start(f32[8,256,128]{2,1,0:T(8,128)} %get-tuple-element.2) | copy-start | bytes 3145732
  89.4 13.6 %copy-start.7 = (f32[1024,128]{1,0:T(8,128)S(1)}, f32[1024,128]{1,0:T(8,128)}, u32[]{:S(2)}) copy-start(f32[1024,128]{1,0:T(8,128)} %fusion.12) | copy-start | bytes 1572868
  111.1 98.9 %all-reduce.3.cloned.1.call-start = ((), (), s32[]{:S(2)}) async-start(), calls=%async_computation.3 | async-start | bytes 131072 | tf_op jit(solution)/shard_map/psum | solution.py:12
  138.8 105.1 %all-reduce.5.cloned.1.call-start = ((), (), s32[]{:S(2)}) async-start(), calls=%async_computation.4 | async-start | bytes 131072 | tf_op jit(solution)/shard_map/psum | solution.py:12
  210.1 335.3 %reduce-scatter.5.cloned.1.call-start = ((), (), s32[]{:S(2)}) async-start(), calls=%async_computation.5 | async-start | bytes 9437184 | tf_op jit(solution)/shard_map/reduce_scatter | solution.py:68
  269.7 23.0 %slice-start.4 = ((s8[8388608]{0:T(1024)(128)(4,1)}), s8[4194304]{0:T(1024)(128)(4,1)S(1)}, s32[]{:S(2)}) async-start(s8[8388608]{0:T(1024)(128)(4,1)} %bitcast.64), calls=%async_computation.10 | async-start | bytes 8388608
  276.8 15.9 %slice-start.5 = ((s8[8388608]{0:T(1024)(128)(4,1)}), s8[4194304]{0:T(1024)(128)(4,1)S(1)}, s32[]{:S(2)}) async-start(s8[8388608]{0:T(1024)(128)(4,1)} %bitcast.64), calls=%async_computation.11 | async-start | bytes 8388608
  276.8 30.2 %slice-start.8 = ((s8[8388608]{0:T(1024)(128)(4,1)}), s8[4194304]{0:T(1024)(128)(4,1)S(1)}, s32[]{:S(2)}) async-start(s8[8388608]{0:T(1024)(128)(4,1)} %bitcast.68), calls=%async_computation.14 | async-start | bytes 8388608
  292.7 14.3 %slice-start.9 = ((s8[8388608]{0:T(1024)(128)(4,1)}), s8[4194304]{0:T(1024)(128)(4,1)S(1)}, s32[]{:S(2)}) async-start(s8[8388608]{0:T(1024)(128)(4,1)} %bitcast.68), calls=%async_computation.15 | async-start | bytes 8388608
  292.7 28.7 %slice-start.10 = ((s8[8388608]{0:T(1024)(128)(4,1)}), s8[4194304]{0:T(1024)(128)(4,1)S(1)}, s32[]{:S(2)}) async-start(s8[8388608]{0:T(1024)(128)(4,1)} %bitcast.70), calls=%async_computation.16 | async-start | bytes 8388608
  307.0 14.5 %slice-start.11 = ((s8[8388608]{0:T(1024)(128)(4,1)}), s8[4194304]{0:T(1024)(128)(4,1)S(1)}, s32[]{:S(2)}) async-start(s8[8388608]{0:T(1024)(128)(4,1)} %bitcast.70), calls=%async_computation.17 | async-start | bytes 8388608
  307.0 28.7 %slice-start.12 = ((s8[8388608]{0:T(1024)(128)(4,1)}), s8[4194304]{0:T(1024)(128)(4,1)S(1)}, s32[]{:S(2)}) async-start(s8[8388608]{0:T(1024)(128)(4,1)} %bitcast.72), calls=%async_computation.18 | async-start | bytes 8388608
  321.5 14.2 %slice-start.13 = ((s8[8388608]{0:T(1024)(128)(4,1)}), s8[4194304]{0:T(1024)(128)(4,1)S(1)}, s32[]{:S(2)}) async-start(s8[8388608]{0:T(1024)(128)(4,1)} %bitcast.72), calls=%async_computation.19 | async-start | bytes 8388608
  321.5 28.5 %slice-start.14 = ((s8[8388608]{0:T(1024)(128)(4,1)}), s8[4194304]{0:T(1024)(128)(4,1)S(1)}, s32[]{:S(2)}) async-start(s8[8388608]{0:T(1024)(128)(4,1)} %bitcast.74), calls=%async_computation.20 | async-start | bytes 8388608
  335.7 14.3 %slice-start.15 = ((s8[8388608]{0:T(1024)(128)(4,1)}), s8[4194304]{0:T(1024)(128)(4,1)S(1)}, s32[]{:S(2)}) async-start(s8[8388608]{0:T(1024)(128)(4,1)} %bitcast.74), calls=%async_computation.21 | async-start | bytes 8388608
  335.7 28.7 %slice-start = ((s8[8388608]{0:T(1024)(128)(4,1)}), s8[4194304]{0:T(1024)(128)(4,1)S(1)}, s32[]{:S(2)}) async-start(s8[8388608]{0:T(1024)(128)(4,1)} %bitcast.60), calls=%async_computation.6 | async-start | bytes 8388608
  350.0 14.5 %slice-start.1 = ((s8[8388608]{0:T(1024)(128)(4,1)}), s8[4194304]{0:T(1024)(128)(4,1)S(1)}, s32[]{:S(2)}) async-start(s8[8388608]{0:T(1024)(128)(4,1)} %bitcast.60), calls=%async_computation.7 | async-start | bytes 8388608
  350.0 28.4 %slice-start.18 = ((s8[8388608]{0:T(1024)(128)(4,1)}), s8[4194304]{0:T(1024)(128)(4,1)S(1)}, s32[]{:S(2)}) async-start(s8[8388608]{0:T(1024)(128)(4,1)} %bitcast.78), calls=%async_computation.24 | async-start | bytes 8388608
  364.5 13.9 %slice-start.19 = ((s8[8388608]{0:T(1024)(128)(4,1)}), s8[4194304]{0:T(1024)(128)(4,1)S(1)}, s32[]{:S(2)}) async-start(s8[8388608]{0:T(1024)(128)(4,1)} %bitcast.78), calls=%async_computation.25 | async-start | bytes 8388608
  (2 other events, 13.4 us)
Sparse Core Ops, SparseCore 0:
  111.2 25.5 reduce-scatter.2
  140.8 69.2 all-reduce.2
  212.4 31.4 all-reduce.4
  397.3 148.0 reduce-scatter.4
